TPU v7x, 32 devices: a whole 2x2x4 slice. The times are simulated.
32 devices in a mesh: comp: 2 (over x), gy: 4 (over y, core), gx: 4 (over z).
Axes of the slice: x: 2, y: 2, z: 4, core: 2. Of those that a mesh axis runs over, the one named last changes fastest.
Arguments:
- state: float32 [2, 8, 512, 512], P('comp', None, 'gy', 'gx'), may hold values from -6 to 6
- target: float32 [2, 8, 512, 512], P('comp', None, 'gy', 'gx'), may hold values from -2.5 to 0.5
- land_mask: int32 [2, 512, 512], P('comp', 'gy', 'gx'), may hold values 0 or 1
- diffusivity: float32 [2, 8], replicated, may hold values from 0.03 to 0.24
- coupling: float32 [2, 8, 4], replicated, may hold values from -3 to 3
- w_in: bfloat16 [16, 256], replicated, may hold values from -1.5 to 1.5
- b_in: float32 [256], replicated, may hold values from -3 to 3
- w_mid: bfloat16 [256, 256], replicated, may hold values from -0.375 to 0.375
- b_mid: float32 [256], replicated, may hold values from -3 to 3
- w_out: bfloat16 [256, 4], replicated, may hold values from -0.375 to 0.375
- b_out: float32 [4], replicated, may hold values from -3 to 3
- remap_weight: bfloat16 [2, 4, 4, 16, 4, 128, 128], P('comp', 'gy', 'gx'), may hold values from -0.5 to 0.5
- remap_source: int32 [2, 4, 4, 16, 4], P('comp', 'gy', 'gx'), may hold values from 0 to 127
- remap_target: int32 [2, 4, 4, 16, 4], P('comp', 'gy', 'gx'), may hold values from 0 to 127
- remap_count: int32 [2, 4, 4, 16], P('comp', 'gy', 'gx'), may hold values from 0 to 4, as said below
Outputs:
- new_state: float32 [2, 8, 512, 512], P('comp', None, 'gy', 'gx')
- state_adjoint: float32 [2, 8, 512, 512], P('comp', None, 'gy', 'gx')
- grad_w_in: float32 [16, 256], replicated
- grad_b_in: float32 [256], replicated
- grad_w_mid: float32 [256, 256], replicated
- grad_b_mid: float32 [256], replicated
- grad_w_out: float32 [256, 4], replicated
- grad_b_out: float32 [4], replicated
Inputs may be any that keep to these rules, and one draw needn't show every extreme that they name: remap_count[c, i, j, q] leading slots of the pair are in use, the rest are padding. A pair has slots in use exactly where receiving tile q lies within 2 tile rows of i and in a tile column within 2 of j (periodic), or, for a sender in the top tile row, where q lies in the top tile row within 1 column (periodic) of column 3 - j; such pairs use 1 slot or more; for each component one receiving tile has all 4 slots in use from every such sending tile.
All inputs are finite; a program needn't handle non-finite values. No bound on the sum of `land_mask` on one device may be relied on, other than what follows from the above.
Results may differ from a plain program's by a relative error of at most 0.0037.
Values may be sent and summed in bfloat16 or wider, within the bound.
No kernel may reach another device: no remote copies, remote signals or barrier semaphores. Data moves between devices by JAX's collectives and lax.ppermute only.
A program may use at most 64 MiB of HBM per device.

v0:
```python
import math
import jax
import jax.numpy as jnp
from jax import lax
from jax.sharding import PartitionSpec as P

PRECISE = lax.Precision.HIGHEST


def extended(cells, sides, width, closed):
    for axis, dim in sides:
        count = lax.axis_size(axis)
        ends = count if closed else count - 1
        head = lax.slice_in_dim(cells, 0, width, axis=dim)
        tail = lax.slice_in_dim(cells, cells.shape[dim] - width, cells.shape[dim], axis=dim)
        cells = jnp.concatenate(
            [
                lax.ppermute(tail, axis, [(i, (i + 1) % count) for i in range(ends)]),
                cells,
                lax.ppermute(head, axis, [((i + 1) % count, i) for i in range(ends)]),
            ],
            axis=dim,
        )
    return cells


def partner(block, axis, stride):
    count = lax.axis_size(axis)
    route = []
    for low in range(count):
        high = low | 1 << stride
        if high != low and high < count:
            route += [(low, high), (high, low)]
    return lax.ppermute(block, axis, route)


def silu_slope(preact):
    sigmoid_value = jax.nn.sigmoid(preact)
    return sigmoid_value * (1.0 + preact * (1.0 - sigmoid_value))


def laplace(surface, on_fold):
    wide_field = extended(surface, (("gx", 2),), 1, True)
    tall_field = extended(surface, (("gy", 1),), 1, False)
    top_row = surface[:, -1, :]
    mirrored = top_row[:, ::-1]
    for bit_index in range(lax.axis_size("gx").bit_length() - 1):
        mirrored = partner(mirrored, "gx", bit_index)
    north_rows = tall_field[:, 2:, :]
    north_rows = north_rows.at[:, -1, :].add(jnp.where(on_fold, mirrored, 0.0))
    return (
        wide_field[:, :, 2:]
        + wide_field[:, :, :-2]
        + tall_field[:, :-2, :]
        + north_rows
        - 4.0 * surface
    )


def forward_route(outgoing):
    relayed = lax.all_to_all(outgoing, ("gy", "gx"), split_axis=0, concat_axis=0, tiled=True)
    arrived = partner(relayed, "comp", 0)
    return arrived


def return_route(outgoing):
    relayed = lax.all_to_all(outgoing, ("gy", "gx"), split_axis=0, concat_axis=0, tiled=True)
    arrived = partner(relayed, "comp", 0)
    return arrived


def shards(
    state,
    target,
    land_mask,
    diffusivity,
    coupling,
    w_in,
    b_in,
    w_mid,
    b_mid,
    w_out,
    b_out,
    remap_weight,
    remap_source,
    remap_target,
    remap_count,
):
    comp_index = lax.axis_index("comp")
    is_ocean = comp_index == 1
    on_fold = jnp.logical_and(is_ocean, lax.axis_index("gy") == lax.axis_size("gy") - 1)
    surface = state[0]
    channels, tile_rows, tile_width = surface.shape
    cell_count = tile_rows * tile_width
    peer_count = remap_source.shape[3]
    slot_count = remap_source.shape[4]
    pair_count = peer_count * slot_count
    wet_mask = land_mask[0].astype(jnp.float32).reshape(1, cell_count)
    diff_mask = jnp.where(is_ocean, wet_mask, 1.0)
    diffuse_rate = diffusivity[comp_index]
    couple = coupling[comp_index]
    rounded = surface.astype(jnp.bfloat16)
    source = remap_source[0, 0, 0].reshape(pair_count)
    kernels = remap_weight[0, 0, 0].reshape(pair_count, tile_width, tile_width)
    slot_index = lax.broadcasted_iota(jnp.int32, (peer_count, slot_count), 1)
    live_mask = (
        (slot_index < remap_count[0, 0, 0][:, None]).astype(jnp.float32).reshape(pair_count, 1, 1)
    )
    picked = rounded[:, source, :]
    outgoing = (
        jnp.einsum("cki,kij->kcj", picked, kernels, preferred_element_type=jnp.float32) * live_mask
    )
    arrived = forward_route(outgoing.reshape(peer_count, slot_count, channels, tile_width))
    laplacian = laplace(surface, on_fold).reshape(channels, cell_count)
    row_index = lax.broadcasted_iota(jnp.int32, (tile_rows, pair_count), 0)
    landing = (row_index == remap_target[0, 0, 0].reshape(1, pair_count)).astype(jnp.float32)
    remapped = jnp.einsum(
        "tk,kcj->ctj", landing, arrived.reshape(pair_count, channels, tile_width), precision=PRECISE
    )
    own_fields = rounded.reshape(channels, cell_count)
    other_fields = remapped.astype(jnp.bfloat16).reshape(channels, cell_count)
    features = jnp.concatenate(
        [
            jnp.where(is_ocean, other_fields, own_fields),
            jnp.where(is_ocean, own_fields, other_fields),
        ],
        axis=0,
    )
    current = surface.reshape(channels, cell_count)
    goal = target[0].reshape(channels, cell_count)
    block_size = math.gcd(cell_count, 2048)

    def advance(block_index, loop_state):
        new_fields, misfits, feature_cots, gradients = loop_state
        offset = block_index * block_size

        def take_block(array):
            return lax.dynamic_slice_in_dim(array, offset, block_size, 1)

        feature_block = take_block(features)
        wet_block = take_block(wet_mask)
        diff_block = take_block(diff_mask)
        pre_first = (
            jnp.einsum("fh,fn->hn", w_in, feature_block, preferred_element_type=jnp.float32)
            + b_in[:, None]
        )
        hidden_first = jax.nn.silu(pre_first).astype(jnp.bfloat16)
        pre_second = (
            jnp.einsum("hk,hn->kn", w_mid, hidden_first, preferred_element_type=jnp.float32)
            + b_mid[:, None]
        )
        hidden_second = jax.nn.silu(pre_second).astype(jnp.bfloat16)
        fluxes = (
            jnp.einsum("ho,hn->on", w_out, hidden_second, preferred_element_type=jnp.float32)
            + b_out[:, None]
        ) * wet_block
        updated = (
            take_block(current)
            + diffuse_rate[:, None] * diff_block * take_block(laplacian)
            + jnp.dot(couple, fluxes, precision=PRECISE)
        )
        misfit = updated - take_block(goal)
        flux_cot = (wet_block * jnp.dot(couple.T, misfit, precision=PRECISE)).astype(jnp.bfloat16)
        second_cot = (
            jnp.einsum("ho,on->hn", w_out, flux_cot, preferred_element_type=jnp.float32)
            * silu_slope(pre_second)
        ).astype(jnp.bfloat16)
        first_cot = (
            jnp.einsum("hk,kn->hn", w_mid, second_cot, preferred_element_type=jnp.float32)
            * silu_slope(pre_first)
        ).astype(jnp.bfloat16)
        feature_cot = jnp.einsum("fh,hn->fn", w_in, first_cot, preferred_element_type=jnp.float32)
        additions = (
            jnp.einsum("fn,hn->fh", feature_block, first_cot, preferred_element_type=jnp.float32),
            jnp.sum(first_cot.astype(jnp.float32), axis=1),
            jnp.einsum("hn,kn->hk", hidden_first, second_cot, preferred_element_type=jnp.float32),
            jnp.sum(second_cot.astype(jnp.float32), axis=1),
            jnp.einsum("hn,on->ho", hidden_second, flux_cot, preferred_element_type=jnp.float32),
            jnp.sum(flux_cot.astype(jnp.float32), axis=1),
        )
        new_fields = lax.dynamic_update_slice_in_dim(new_fields, updated, offset, 1)
        misfits = lax.dynamic_update_slice_in_dim(misfits, misfit, offset, 1)
        feature_cots = lax.dynamic_update_slice_in_dim(feature_cots, feature_cot, offset, 1)
        return (new_fields, misfits, feature_cots, jax.tree.map(jnp.add, gradients, additions))

    initial = (
        jnp.zeros((channels, cell_count), jnp.float32),
        jnp.zeros((channels, cell_count), jnp.float32),
        jnp.zeros((2 * channels, cell_count), jnp.float32),
        (
            jnp.zeros(w_in.shape, jnp.float32),
            jnp.zeros(b_in.shape, jnp.float32),
            jnp.zeros(w_mid.shape, jnp.float32),
            jnp.zeros(b_mid.shape, jnp.float32),
            jnp.zeros(w_out.shape, jnp.float32),
            jnp.zeros(b_out.shape, jnp.float32),
        ),
    )
    new_fields, misfits, feature_cots, gradients = lax.fori_loop(
        0, cell_count // block_size, advance, initial
    )
    back_lap = laplace((diff_mask * misfits).reshape(channels, tile_rows, tile_width), on_fold)
    own_cot = jnp.where(is_ocean, feature_cots[channels:], feature_cots[:channels]).reshape(
        channels, tile_rows, tile_width
    )
    other_cot = jnp.where(is_ocean, feature_cots[:channels], feature_cots[channels:]).reshape(
        channels, tile_rows, tile_width
    )
    going_back = jnp.einsum("tk,ctj->kcj", landing, other_cot, precision=PRECISE).astype(
        jnp.bfloat16
    )
    returned = return_route(going_back.reshape(peer_count, slot_count, channels, tile_width))
    spread = (
        jnp.einsum(
            "kcj,kij->kci",
            returned.reshape(pair_count, channels, tile_width),
            kernels,
            preferred_element_type=jnp.float32,
        )
        * live_mask
    )
    anchor = (row_index == source.reshape(1, pair_count)).astype(jnp.float32)
    remap_back = jnp.einsum("tk,kci->cti", anchor, spread, precision=PRECISE)
    adjoint_field = (
        misfits.reshape(channels, tile_rows, tile_width)
        + diffuse_rate[:, None, None] * back_lap
        + own_cot
        + remap_back
    )
    grad_first, bias_first, grad_second, bias_second, grad_third, bias_third = gradients
    grad_first, bias_first, grad_second, bias_second, grad_third, bias_third = lax.psum(
        (grad_first, bias_first, grad_second, bias_second, grad_third, bias_third),
        ("comp", "gy", "gx"),
    )
    scale = 1.0 / (cell_count * lax.axis_size("gy") * lax.axis_size("gx"))
    return (
        new_fields.reshape(1, channels, tile_rows, tile_width),
        adjoint_field.reshape(1, channels, tile_rows, tile_width),
        grad_first * scale,
        bias_first * scale,
        grad_second * scale,
        bias_second * scale,
        grad_third * scale,
        bias_third * scale,
    )


def solution(mesh):
    placed = (
        P("comp", None, "gy", "gx"),
        P("comp", None, "gy", "gx"),
        P("comp", "gy", "gx"),
        P(),
        P(),
        P(),
        P(),
        P(),
        P(),
        P(),
        P(),
        P("comp", "gy", "gx", None, None, None, None),
        P("comp", "gy", "gx", None, None),
        P("comp", "gy", "gx", None, None),
        P("comp", "gy", "gx", None),
    )
    return jax.shard_map(
        shards,
        mesh=mesh,
        in_specs=placed,
        out_specs=(
            P("comp", None, "gy", "gx"),
            P("comp", None, "gy", "gx"),
            P(),
            P(),
            P(),
            P(),
            P(),
            P(),
        ),
        check_vma=False,
    )
```

profile of v0, /device:TPU:0, one launch (start us, length us, event | category | flops | bytes accessed | tf_op | source)
XLA Modules:
  0.0 382.0 jit_solution(18036116100139440150)
XLA Ops:
  10.0 3.1 collective-permute-start.4
  14.3 3.8 %collective-permute-start.2 = (f32[8,1,128]{1,2,0:T(8,128)}, f32[8,1,128]{1,2,0:T(8,128)}, u32[]{:S(2)}, u32[]{:S(2)}) collective-permute-start(f32[8,1,128]{1,2,0:T(8,128)} %get-tuple-element.628), channel_id=1, source_target_pairs={{0,4},{4,8},{8,12},{1,5},{5,9},{9,13},{2,6},{6,10},{10,14},{3,7},{... | collective-permute-start | bytes 12296 | tf_op jit(solution)/shard_map/ppermute | solution.py:18
  18.1 2.5 collective-permute-start
  25.0 6.2 %all-to-all-start = ((f32[16,4,8,128]{3,2,1,0:T(8,128)}), f32[16,4,8,128]{3,2,1,0:T(8,128)}, u32[]{:S(2)}, u32[]{:S(2)}) async-start(f32[16,4,8,128]{3,2,1,0:T(8,128)} %bitcast.7), calls=%async_computation | async-start | bytes 524288 | tf_op jit(solution)/shard_map/all_to_all | solution.py:61
  32.8 2.8 collective-permute-start.5
  37.8 3.1 collective-permute-done.5
  44.0 2.7 scatter-add.6
  51.9 2.6 copy_bitcast_fusion.4
  54.5 3.9 %collective-permute-done.6 = f32[16,4,8,128]{3,2,1,0:T(8,128)S(1)} collective-permute-done((f32[16,4,8,128]{3,2,1,0:T(8,128)}, f32[16,4,8,128]{3,2,1,0:T(8,128)S(1)}, u32[]{:S(2)}, u32[]{:S(2)}) %collective-permute-start.6) | collective-permute-done | bytes 262176 | tf_op jit(solution)/shard_map/ppermute | solution.py:34
  62.6 104.6 %while.32 = (s32[]{:T(128)}, f32[8,16384]{1,0:T(8,128)}, f32[8,16384]{1,0:T(8,128)}, f32[16,16384]{1,0:T(8,128)}, f32[16,256]{1,0:T(8,128)S(1)}, /*index=5*/f32[...) while((s32[]{:T(128)}, f32[8,16384]{1,0:T(8,128)}, ...), condition=%wide.region_4.5_spmd.clone, body=%wide.region_0.4_spmd.clone.sunk | while | flops 890530304 | bytes 47954832 | solution.py:199
  69.7 2.7 convert_reduce_fusion.7
  82.8 2.7 convert_reduce_fusion.7
  95.9 2.7 convert_reduce_fusion.7
  108.9 2.7 convert_reduce_fusion.7
  122.0 2.7 convert_reduce_fusion.7
  135.1 2.7 convert_reduce_fusion.7
  148.2 2.7 convert_reduce_fusion.7
  161.2 2.7 convert_reduce_fusion.7
  170.0 38.8 %all-reduce = (f32[16,256]{1,0:T(8,128)S(1)}, f32[256]{0:T(256)S(1)}, f32[256]{0:T(256)S(1)}, f32[256,4]{0,1:T(4,128)S(1)}, f32[4]{0:T(128)S(1)}) all-reduce(f32[16,256]{1,0:T(8,128)S(1)} %get-tuple-element.422, f32[256]{0:T(256)S(1)} %get-tuple-element.423, ...), channel_id=1, replica_groups=mesh['comp'=2,'gy'=4,'gx'=4] {'comp','gy','gx'}, use_global_device_ids=true, to_apply=%region_5.6 | all-reduce | flops 5636 | bytes 45088 | tf_op jit(solution)/shard_map/psum | solution.py:231
  214.9 3.8 %collective-permute-start.9 = (f32[8,1,128]{1,2,0:T(8,128)}, f32[8,1,128]{1,2,0:T(8,128)}, u32[]{:S(2)}, u32[]{:S(2)}) collective-permute-start(f32[8,1,128]{1,2,0:T(8,128)} %get-tuple-element.623), channel_id=1, source_target_pairs={{0,4},{4,8},{8,12},{1,5},{5,9},{9,13},{2,6},{6,10},{10,14},{3,7},{... | collective-permute-start | bytes 12296 | tf_op jit(solution)/shard_map/ppermute | solution.py:18
  224.2 7.0 %all-to-all-start.1 = ((bf16[16,4,8,128]{3,1,2,0:T(4,128)(2,1)}), bf16[16,4,8,128]{3,1,2,0:T(4,128)(2,1)S(1)}, u32[]{:S(2)}, u32[]{:S(2)}) async-start(bf16[16,4,8,128]{3,1,2,0:T(4,128)(2,1)} %copy.141), calls=%async_computation.1 | async-start | bytes 262144 | tf_op jit(solution)/shard_map/all_to_all | solution.py:67
  240.3 2.9 collective-permute-start.12
  250.8 116.6 %all-reduce.3.cloned.1.call-done = f32[256,256]{1,0:T(8,128)} async-done(((f32[256,256]{1,0:T(8,128)}), f32[256,256]{1,0:T(8,128)}) %all-reduce.3.cloned.1.call-update) | async-done | bytes 262160 | tf_op jit(solution)/shard_map/psum | solution.py:231
  370.4 2.7 fusion.18
  (368 shorter events, 142.1 us)
Async XLA Ops:
  7.2 16.4 %copy-start = (bf16[1,1,1,16,4,128,128]{6,5,4,3,2,1,0:T(8,128)(2,1)S(1)}, bf16[1,1,1,16,4,128,128]{6,5,4,3,2,1,0:T(8,128)(2,1)}, u32[]{:S(2)}) copy-start(bf16[1,1,1,16,4,128,128]{6,5,4,3,2,1,0:T(8,128)(2,1)} %param.32) | copy-start | bytes 6291460
  7.2 14.5 %copy-start.16 = (s32[1,1,1,16,4]{3,4,2,1,0:T(4,128)S(1)}, s32[1,1,1,16,4]{3,4,2,1,0:T(4,128)}, u32[]{:S(2)}) copy-start(s32[1,1,1,16,4]{3,4,2,1,0:T(4,128)} %param.33) | copy-start | bytes 772
  7.2 14.6 %copy-start.19 = (s32[1,1,1,16]{3,2,1,0:T(1,128)S(1)}, s32[1,1,1,16]{3,2,1,0:T(1,128)}, u32[]{:S(2)}) copy-start(s32[1,1,1,16]{3,2,1,0:T(1,128)} %param.35) | copy-start | bytes 196
  10.0 22.8 %collective-permute-start.4 = (f32[8,128]{1,0:T(8,128)S(1)}, f32[8,128]{1,0:T(8,128)S(1)}, u32[]{:S(2)}, u32[]{:S(2)}) collective-permute-start(f32[8,128]{1,0:T(8,128)S(1)} %rev.6), channel_id=1, source_target_pairs={{0,1},{1,0},{2,3},{3,2},{4,5},{5,4},{6,7},{7,6},{8,9},{9,8},{10,11... | collective-permute-start | bytes 12296 | tf_op jit(solution)/shard_map/ppermute | solution.py:34
  13.0 22.6 %collective-permute-start.3 = (f32[8,1,128]{1,2,0:T(8,128)}, f32[8,1,128]{1,2,0:T(8,128)}, u32[]{:S(2)}, u32[]{:S(2)}) collective-permute-start(f32[8,1,128]{1,2,0:T(8,128)} %get-tuple-element.630), channel_id=1, source_target_pairs={{4,0},{8,4},{12,8},{5,1},{9,5},{13,9},{6,2},{10,6},{14,10},{7,3},{... | collective-permute-start | bytes 12296 | tf_op jit(solution)/shard_map/ppermute | solution.py:20
  14.3 32.4 %collective-permute-start.2 = (f32[8,1,128]{1,2,0:T(8,128)}, f32[8,1,128]{1,2,0:T(8,128)}, u32[]{:S(2)}, u32[]{:S(2)}) collective-permute-start(f32[8,1,128]{1,2,0:T(8,128)} %get-tuple-element.628), channel_id=1, source_target_pairs={{0,4},{4,8},{8,12},{1,5},{5,9},{9,13},{2,6},{6,10},{10,14},{3,7},{... | collective-permute-start | bytes 12296 | tf_op jit(solution)/shard_map/ppermute | solution.py:18
  18.1 28.6 %collective-permute-start = (f32[8,128,1]{1,2,0:T(1,128)S(1)}, f32[8,128,1]{1,2,0:T(1,128)S(1)}, u32[]{:S(2)}, u32[]{:S(2)}) collective-permute-start(f32[8,128,1]{1,2,0:T(1,128)S(1)} %get-tuple-element.626), channel_id=1, source_target_pairs={{1,0},{2,1},{3,2},{0,3},{5,4},{6,5},{7,6},{4,7},{9,8},{10,9},{11,1... | collective-permute-start | bytes 12296 | tf_op jit(solution)/shard_map/ppermute | solution.py:20
  20.7 26.1 %collective-permute-start.1 = (f32[8,128,1]{1,2,0:T(1,128)S(1)}, f32[8,128,1]{1,2,0:T(1,128)S(1)}, u32[]{:S(2)}, u32[]{:S(2)}) collective-permute-start(f32[8,128,1]{1,2,0:T(1,128)S(1)} %get-tuple-element.627), channel_id=1, source_target_pairs={{0,1},{1,2},{2,3},{3,0},{4,5},{5,6},{6,7},{7,4},{8,9},{9,10},{10,1... | collective-permute-start | bytes 12296 | tf_op jit(solution)/shard_map/ppermute | solution.py:18
  20.7 10.5 %copy-start.22 = (f32[2,8]{1,0:T(2,128)S(1)}, f32[2,8]{1,0:T(2,128)}, u32[]{:S(2)}) copy-start(f32[2,8]{1,0:T(2,128)} %param.24) | copy-start | bytes 196
  20.7 10.5 %copy-start.12 = (s32[1,128,128]{2,1,0:T(8,128)S(1)}, s32[1,128,128]{2,1,0:T(8,128)}, u32[]{:S(2)}) copy-start(s32[1,128,128]{2,1,0:T(8,128)} %param.23) | copy-start | bytes 196612
  20.7 10.7 %copy-start.3 = (f32[1,8,128,128]{3,2,1,0:T(8,128)S(1)}, f32[1,8,128,128]{3,2,1,0:T(8,128)}, u32[]{:S(2)}) copy-start(f32[1,8,128,128]{3,2,1,0:T(8,128)} %param.21) | copy-start | bytes 1572868
  25.0 25.3 %all-to-all-start = ((f32[16,4,8,128]{3,2,1,0:T(8,128)}), f32[16,4,8,128]{3,2,1,0:T(8,128)}, u32[]{:S(2)}, u32[]{:S(2)}) async-start(f32[16,4,8,128]{3,2,1,0:T(8,128)} %bitcast.7), calls=%async_computation | async-start | bytes 524288 | tf_op jit(solution)/shard_map/all_to_all | solution.py:61
  32.8 8.1 %collective-permute-start.5 = (f32[8,128]{1,0:T(8,128)S(1)}, f32[8,128]{1,0:T(8,128)S(1)}, u32[]{:S(2)}, u32[]{:S(2)}) collective-permute-start(f32[8,128]{1,0:T(8,128)S(1)} %collective-permute-done.4), channel_id=1, source_target_pairs={{0,2},{2,0},{1,3},{3,1},{4,6},{6,4},{5,7},{7,5},{8,10},{10,8},{9,1... | collective-permute-start | bytes 12296 | tf_op jit(solution)/shard_map/ppermute | solution.py:34
  50.3 8.1 %collective-permute-start.6 = (f32[16,4,8,128]{3,2,1,0:T(8,128)}, f32[16,4,8,128]{3,2,1,0:T(8,128)S(1)}, u32[]{:S(2)}, u32[]{:S(2)}) collective-permute-start(f32[16,4,8,128]{3,2,1,0:T(8,128)} %all-to-all-done), channel_id=1, source_target_pairs={{0,16},{16,0},{1,17},{17,1},{2,18},{18,2},{3,19},{19,3},{4,20},{20... | collective-permute-start | bytes 786440 | tf_op jit(solution)/shard_map/ppermute | solution.py:34
  211.8 28.5 %collective-permute-start.11 = (f32[8,128]{1,0:T(8,128)S(1)}, f32[8,128]{1,0:T(8,128)S(1)}, u32[]{:S(2)}, u32[]{:S(2)}) collective-permute-start(f32[8,128]{1,0:T(8,128)S(1)} %rev.7), channel_id=1, source_target_pairs={{0,1},{1,0},{2,3},{3,2},{4,5},{5,4},{6,7},{7,6},{8,9},{9,8},{10,11... | collective-permute-start | bytes 12296 | tf_op jit(solution)/shard_map/ppermute | solution.py:34
  213.6 29.6 %collective-permute-start.10 = (f32[8,1,128]{1,2,0:T(8,128)}, f32[8,1,128]{1,2,0:T(8,128)}, u32[]{:S(2)}, u32[]{:S(2)}) collective-permute-start(f32[8,1,128]{1,2,0:T(8,128)} %get-tuple-element.625), channel_id=1, source_target_pairs={{4,0},{8,4},{12,8},{5,1},{9,5},{13,9},{6,2},{10,6},{14,10},{7,3},{... | collective-permute-start | bytes 12296 | tf_op jit(solution)/shard_map/ppermute | solution.py:20
  214.9 155.4 %collective-permute-start.9 = (f32[8,1,128]{1,2,0:T(8,128)}, f32[8,1,128]{1,2,0:T(8,128)}, u32[]{:S(2)}, u32[]{:S(2)}) collective-permute-start(f32[8,1,128]{1,2,0:T(8,128)} %get-tuple-element.623), channel_id=1, source_target_pairs={{0,4},{4,8},{8,12},{1,5},{5,9},{9,13},{2,6},{6,10},{10,14},{3,7},{... | collective-permute-start | bytes 12296 | tf_op jit(solution)/shard_map/ppermute | solution.py:18
  218.7 151.6 %collective-permute-start.7 = (f32[8,128,1]{1,2,0:T(1,128)S(1)}, f32[8,128,1]{1,2,0:T(1,128)S(1)}, u32[]{:S(2)}, u32[]{:S(2)}) collective-permute-start(f32[8,128,1]{1,2,0:T(1,128)S(1)} %get-tuple-element.621), channel_id=1, source_target_pairs={{1,0},{2,1},{3,2},{0,3},{5,4},{6,5},{7,6},{4,7},{9,8},{10,9},{11,1... | collective-permute-start | bytes 12296 | tf_op jit(solution)/shard_map/ppermute | solution.py:20
  221.0 149.4 %collective-permute-start.8 = (f32[8,128,1]{1,2,0:T(1,128)S(1)}, f32[8,128,1]{1,2,0:T(1,128)S(1)}, u32[]{:S(2)}, u32[]{:S(2)}) collective-permute-start(f32[8,128,1]{1,2,0:T(1,128)S(1)} %get-tuple-element.622), channel_id=1, source_target_pairs={{0,1},{1,2},{2,3},{3,0},{4,5},{5,6},{6,7},{7,4},{8,9},{9,10},{10,1... | collective-permute-start | bytes 12296 | tf_op jit(solution)/shard_map/ppermute | solution.py:18
  223.1 12.3 %copy-start.4 = (f32[8,16384]{1,0:T(8,128)S(1)}, f32[8,16384]{1,0:T(8,128)}, u32[]{:S(2)}) copy-start(f32[8,16384]{1,0:T(8,128)} %get-tuple-element.420) | copy-start | bytes 1572868
  224.2 26.0 %all-to-all-start.1 = ((bf16[16,4,8,128]{3,1,2,0:T(4,128)(2,1)}), bf16[16,4,8,128]{3,1,2,0:T(4,128)(2,1)S(1)}, u32[]{:S(2)}, u32[]{:S(2)}) async-start(bf16[16,4,8,128]{3,1,2,0:T(4,128)(2,1)} %copy.141), calls=%async_computation.1 | async-start | bytes 262144 | tf_op jit(solution)/shard_map/all_to_all | solution.py:67
  231.2 136.2 %all-reduce.3.cloned.1.call-start = ((), (), s32[]{:S(2)}) async-start(), calls=%async_computation.2 | async-start | bytes 524288 | tf_op jit(solution)/shard_map/psum | solution.py:231
  240.3 4.6 %collective-permute-start.12 = (f32[8,128]{1,0:T(8,128)S(1)}, f32[8,128]{1,0:T(8,128)S(1)}, u32[]{:S(2)}, u32[]{:S(2)}) collective-permute-start(f32[8,128]{1,0:T(8,128)S(1)} %collective-permute-done.11), channel_id=1, source_target_pairs={{0,2},{2,0},{1,3},{3,1},{4,6},{6,4},{5,7},{7,5},{8,10},{10,8},{9,1... | collective-permute-start | bytes 12296 | tf_op jit(solution)/shard_map/ppermute | solution.py:34
  250.2 118.9 %collective-permute-start.13 = (bf16[16,4,8,128]{3,1,2,0:T(4,128)(2,1)S(1)}, bf16[16,4,8,128]{3,1,2,0:T(4,128)(2,1)S(1)}, u32[]{:S(2)}, u32[]{:S(2)}) collective-permute-start(bf16[16,4,8,128]{3,1,2,0:T(4,128)(2,1)S(1)} %all-to-all-done.1), channel_id=1, source_target_pairs={{0,16},{16,0},{1,17},{17,1},{2,18},{18,2},{3,19},{19,3},{4,20},{20... | collective-permute-start | bytes 393224 | tf_op jit(solution)/shard_map/ppermute | solution.py:34
  (73 other events, 155.0 us)
Sparse Core Ops, SparseCore 0:
  240.4 126.9 all-reduce.2
where the time goes:
time: 384 us; the launch traced here: 382 us
  waiting for transfers between devices  124 us (32%)
  matrix products  105 us (27%)
  starting transfers between devices  41.2 us (11%)
  local copies, waits for them, and re-layouts  38.9 us (10%)
  blocking collectives  38.8 us (10%)
  other arithmetic  18.7 us (5%)
  between operations  14.5 us (4%)
    psum x1, waiting for transfers between devices, shards(): lax.psum((grad_first, bias_first, grad_second, bias_second, grad_third, b...  117 us
    psum x1, blocking collectives, shards(): lax.psum((grad_first, bias_first, grad_second, bias_second, grad_third, b...  38.8 us
    dot_general x8, matrix products, advance(): jnp.einsum('ho,on->hn', w_out, flux_cot, preferred_element_type=jnp.float32)  21.6 us
    dot_general x8, matrix products, advance(): jnp.einsum('hk,hn->kn', w_mid, hidden_first, preferred_element_type=jnp.f...  18.9 us
    dot_general x8, matrix products, advance(): jnp.dot(couple, fluxes, precision=PRECISE)  14.6 us
    ppermute x6, starting transfers between devices, partner(): return lax.ppermute(block, axis, route)  12.7 us
    unnamed x41, local copies, waits for them, and re-layouts  9.63 us
    dot_general x8, matrix products, advance(): jnp.dot(couple.T, misfit, precision=PRECISE)  9.23 us
  transfers between devices with their start and end apart: 17, of which 4 were waited for; matrix products, arithmetic and copies ran while one was open for 11% of the time, Pallas kernels for 0%

commit v1 on v0

--- a/solution.py
+++ b/solution.py
@@ -229,8 +229,10 @@
     )
     grad_first, bias_first, grad_second, bias_second, grad_third, bias_third = gradients
     grad_first, bias_first, grad_second, bias_second, grad_third, bias_third = lax.psum(
-        (grad_first, bias_first, grad_second, bias_second, grad_third, bias_third),
-        ("comp", "gy", "gx"),
+        lax.psum(
+            (grad_first, bias_first, grad_second, bias_second, grad_third, bias_third), "comp"
+        ),
+        ("gy", "gx"),
     )
     scale = 1.0 / (cell_count * lax.axis_size("gy") * lax.axis_size("gx"))
     return (

time: 384 us -> 392 us (1.021)
  blocking collectives: 38.8 us -> 66.2 us
  waiting for transfers between devices: 124 us -> 109 us
  starting transfers between devices: 41.2 us -> 36.7 us
    psum x1, waiting for transfers between devices: 117 us -> 13.2 us  [shards(): lax.psum((grad_first, bias_first, grad_second, bias_second, grad_third, b...]
    psum x0 -> x1, waiting for transfers between devices: none -> 87.1 us  [shards(): lax.psum(lax.psum((grad_first, bias_first, grad_second, bias_second, grad...]
    psum x0 -> x1, blocking collectives: none -> 57.9 us  [shards(): lax.psum(lax.psum((grad_first, bias_first, grad_second, bias_second, grad...]
    psum x1, blocking collectives: 38.8 us -> 8.28 us  [shards(): lax.psum((grad_first, bias_first, grad_second, bias_second, grad_third, b...]
  transfers between devices with their start and end apart: 17 -> 18, of which waited for: 4 -> 5; matrix products, arithmetic and copies ran while one was open for 11% -> 12% of each run, Pallas kernels for 0% -> 0%
where the time goes in v1:
time: 392 us; the launch traced here: 390 us
  waiting for transfers between devices  109 us (28%)
  matrix products  105 us (27%)
  blocking collectives  66.2 us (17%)
  local copies, waits for them, and re-layouts  38.8 us (10%)
  starting transfers between devices  36.7 us (9%)
  other arithmetic  18.6 us (5%)
  between operations  14.6 us (4%)
    psum x1, waiting for transfers between devices, shards(): lax.psum(lax.psum((grad_first, bias_first, grad_second, bias_second, grad...  87.1 us
    psum x1, blocking collectives, shards(): lax.psum(lax.psum((grad_first, bias_first, grad_second, bias_second, grad...  57.9 us
    dot_general x8, matrix products, advance(): jnp.einsum('ho,on->hn', w_out, flux_cot, preferred_element_type=jnp.float32)  21.6 us
    dot_general x8, matrix products, advance(): jnp.einsum('hk,hn->kn', w_mid, hidden_first, preferred_element_type=jnp.f...  19 us
    dot_general x8, matrix products, advance(): jnp.dot(couple, fluxes, precision=PRECISE)  14.6 us
    psum x1, waiting for transfers between devices, shards(): lax.psum((grad_first, bias_first, grad_second, bias_second, grad_third, b...  13.2 us
    unnamed x41, local copies, waits for them, and re-layouts  9.63 us
    ppermute x6, starting transfers between devices, partner(): return lax.ppermute(block, axis, route)  9.58 us
  transfers between devices with their start and end apart: 18, of which 5 were waited for; matrix products, arithmetic and copies ran while one was open for 12% of the time, Pallas kernels for 0%

profile of v1, /device:TPU:0, one launch (start us, length us, event | category | flops | bytes accessed | tf_op | source)
XLA Modules:
  0.0 389.6 jit_solution(11951899733540797867)
XLA Ops:
  10.0 3.1 collective-permute-start.4
  14.3 3.8 collective-permute-start.2
  25.0 6.2 %all-to-all-start = ((f32[16,4,8,128]{3,2,1,0:T(8,128)}), f32[16,4,8,128]{3,2,1,0:T(8,128)}, u32[]{:S(2)}, u32[]{:S(2)}) async-start(f32[16,4,8,128]{3,2,1,0:T(8,128)} %bitcast.7), calls=%async_computation | async-start | bytes 524288 | tf_op jit(solution)/shard_map/all_to_all | solution.py:61
  32.8 2.8 collective-permute-start.5
  37.8 3.1 collective-permute-done.5
  44.0 2.7 scatter-add.6
  54.5 3.9 %collective-permute-done.6 = f32[16,4,8,128]{3,2,1,0:T(8,128)S(1)} collective-permute-done((f32[16,4,8,128]{3,2,1,0:T(8,128)}, f32[16,4,8,128]{3,2,1,0:T(8,128)S(1)}, u32[]{:S(2)}, u32[]{:S(2)}) %collective-permute-start.6) | collective-permute-done | bytes 262176 | tf_op jit(solution)/shard_map/ppermute | solution.py:34
  62.6 104.7 %while.32 = (s32[]{:T(128)}, f32[8,16384]{1,0:T(8,128)}, f32[8,16384]{1,0:T(8,128)}, f32[16,16384]{1,0:T(8,128)}, f32[16,256]{1,0:T(8,128)S(1)}, /*index=5*/f32[...) while((s32[]{:T(128)}, f32[8,16384]{1,0:T(8,128)}, ...), condition=%wide.region_4.5_spmd.clone, body=%wide.region_0.4_spmd.clone.sunk | while | flops 890530304 | bytes 47954832 | solution.py:199
  69.7 2.7 convert_reduce_fusion.7
  82.8 2.7 convert_reduce_fusion.7
  95.9 2.7 convert_reduce_fusion.7
  109.0 2.7 convert_reduce_fusion.7
  122.1 2.7 convert_reduce_fusion.7
  135.2 2.7 convert_reduce_fusion.7
  148.2 2.7 convert_reduce_fusion.7
  161.3 2.7 convert_reduce_fusion.7
  170.0 8.3 %all-reduce.1 = (f32[16,256]{1,0:T(8,128)S(1)}, f32[256]{0:T(256)S(1)}, f32[256]{0:T(256)S(1)}, f32[256,4]{0,1:T(4,128)S(1)}, f32[4]{0:T(128)S(1)}) all-reduce(f32[16,256]{1,0:T(8,128)S(1)} %get-tuple-element.422, f32[256]{0:T(256)S(1)} %get-tuple-element.423, ...), channel_id=1, replica_groups=mesh['comp'=2,'gy'=4,'gx'=4] {'comp'}, use_global_device_ids=true, to_apply=%region_5.6 | all-reduce | flops 5636 | bytes 45088 | tf_op jit(solution)/shard_map/psum | solution.py:232
  178.3 57.9 %all-reduce = (f32[16,256]{1,0:T(8,128)S(1)}, f32[256]{0:T(256)S(1)}, f32[256]{0:T(256)S(1)}, f32[256,4]{0,1:T(4,128)S(1)}, f32[4]{0:T(128)S(1)}) all-reduce(f32[16,256]{1,0:T(8,128)S(1)} %get-tuple-element.604, f32[256]{0:T(256)S(1)} %get-tuple-element.605, ...), channel_id=1, replica_groups=mesh['comp'=2,'gy'=4,'gx'=4] {'gy','gx'}, use_global_device_ids=true, to_apply=%region_6.7 | all-reduce | flops 5636 | bytes 45088 | tf_op jit(solution)/shard_map/psum | solution.py:231
  243.5 5.4 %all-to-all-start.1 = ((bf16[16,4,8,128]{3,1,2,0:T(4,128)(2,1)}), bf16[16,4,8,128]{3,1,2,0:T(4,128)(2,1)S(1)}, u32[]{:S(2)}, u32[]{:S(2)}) async-start(bf16[16,4,8,128]{3,1,2,0:T(4,128)(2,1)} %copy.141), calls=%async_computation.1 | async-start | bytes 262144 | tf_op jit(solution)/shard_map/all_to_all | solution.py:67
  249.4 3.1 collective-permute-start.9
  252.5 3.4 collective-permute-start.7
  274.8 13.2 %all-reduce.5.cloned.1.call-done = f32[256,256]{1,0:T(8,128)} async-done(((f32[256,256]{1,0:T(8,128)}), f32[256,256]{1,0:T(8,128)}) %all-reduce.5.cloned.1.call-update) | async-done | bytes 262160 | tf_op jit(solution)/shard_map/psum | solution.py:232
  289.3 2.7 fusion.18
  294.1 87.1 %all-reduce.7.cloned.1.call-done = f32[256,256]{1,0:T(8,128)} async-done(((f32[256,256]{1,0:T(8,128)}), f32[256,256]{1,0:T(8,128)}) %all-reduce.7.cloned.1.call-update) | async-done | bytes 262160 | tf_op jit(solution)/shard_map/psum | solution.py:231
  (372 shorter events, 145.6 us)
Async XLA Ops:
  7.2 16.4 %copy-start = (bf16[1,1,1,16,4,128,128]{6,5,4,3,2,1,0:T(8,128)(2,1)S(1)}, bf16[1,1,1,16,4,128,128]{6,5,4,3,2,1,0:T(8,128)(2,1)}, u32[]{:S(2)}) copy-start(bf16[1,1,1,16,4,128,128]{6,5,4,3,2,1,0:T(8,128)(2,1)} %param.32) | copy-start | bytes 6291460
  7.2 14.5 %copy-start.16 = (s32[1,1,1,16,4]{3,4,2,1,0:T(4,128)S(1)}, s32[1,1,1,16,4]{3,4,2,1,0:T(4,128)}, u32[]{:S(2)}) copy-start(s32[1,1,1,16,4]{3,4,2,1,0:T(4,128)} %param.33) | copy-start | bytes 772
  7.2 14.7 %copy-start.19 = (s32[1,1,1,16]{3,2,1,0:T(1,128)S(1)}, s32[1,1,1,16]{3,2,1,0:T(1,128)}, u32[]{:S(2)}) copy-start(s32[1,1,1,16]{3,2,1,0:T(1,128)} %param.35) | copy-start | bytes 196
  10.0 22.8 %collective-permute-start.4 = (f32[8,128]{1,0:T(8,128)S(1)}, f32[8,128]{1,0:T(8,128)S(1)}, u32[]{:S(2)}, u32[]{:S(2)}) collective-permute-start(f32[8,128]{1,0:T(8,128)S(1)} %rev.6), channel_id=1, source_target_pairs={{0,1},{1,0},{2,3},{3,2},{4,5},{5,4},{6,7},{7,6},{8,9},{9,8},{10,11... | collective-permute-start | bytes 12296 | tf_op jit(solution)/shard_map/ppermute | solution.py:34
  13.0 22.6 %collective-permute-start.3 = (f32[8,1,128]{1,2,0:T(8,128)}, f32[8,1,128]{1,2,0:T(8,128)}, u32[]{:S(2)}, u32[]{:S(2)}) collective-permute-start(f32[8,1,128]{1,2,0:T(8,128)} %get-tuple-element.635), channel_id=1, source_target_pairs={{4,0},{8,4},{12,8},{5,1},{9,5},{13,9},{6,2},{10,6},{14,10},{7,3},{... | collective-permute-start | bytes 12296 | tf_op jit(solution)/shard_map/ppermute | solution.py:20
  14.3 32.4 %collective-permute-start.2 = (f32[8,1,128]{1,2,0:T(8,128)}, f32[8,1,128]{1,2,0:T(8,128)}, u32[]{:S(2)}, u32[]{:S(2)}) collective-permute-start(f32[8,1,128]{1,2,0:T(8,128)} %get-tuple-element.633), channel_id=1, source_target_pairs={{0,4},{4,8},{8,12},{1,5},{5,9},{9,13},{2,6},{6,10},{10,14},{3,7},{... | collective-permute-start | bytes 12296 | tf_op jit(solution)/shard_map/ppermute | solution.py:18
  18.1 28.5 %collective-permute-start = (f32[8,128,1]{1,2,0:T(1,128)S(1)}, f32[8,128,1]{1,2,0:T(1,128)S(1)}, u32[]{:S(2)}, u32[]{:S(2)}) collective-permute-start(f32[8,128,1]{1,2,0:T(1,128)S(1)} %get-tuple-element.631), channel_id=1, source_target_pairs={{1,0},{2,1},{3,2},{0,3},{5,4},{6,5},{7,6},{4,7},{9,8},{10,9},{11,1... | collective-permute-start | bytes 12296 | tf_op jit(solution)/shard_map/ppermute | solution.py:20
  20.7 26.0 %collective-permute-start.1 = (f32[8,128,1]{1,2,0:T(1,128)S(1)}, f32[8,128,1]{1,2,0:T(1,128)S(1)}, u32[]{:S(2)}, u32[]{:S(2)}) collective-permute-start(f32[8,128,1]{1,2,0:T(1,128)S(1)} %get-tuple-element.632), channel_id=1, source_target_pairs={{0,1},{1,2},{2,3},{3,0},{4,5},{5,6},{6,7},{7,4},{8,9},{9,10},{10,1... | collective-permute-start | bytes 12296 | tf_op jit(solution)/shard_map/ppermute | solution.py:18
  20.7 10.5 %copy-start.12 = (s32[1,128,128]{2,1,0:T(8,128)S(1)}, s32[1,128,128]{2,1,0:T(8,128)}, u32[]{:S(2)}) copy-start(s32[1,128,128]{2,1,0:T(8,128)} %param.23) | copy-start | bytes 196612
  20.7 10.6 %copy-start.3 = (f32[1,8,128,128]{3,2,1,0:T(8,128)S(1)}, f32[1,8,128,128]{3,2,1,0:T(8,128)}, u32[]{:S(2)}) copy-start(f32[1,8,128,128]{3,2,1,0:T(8,128)} %param.21) | copy-start | bytes 1572868
  25.0 25.3 %all-to-all-start = ((f32[16,4,8,128]{3,2,1,0:T(8,128)}), f32[16,4,8,128]{3,2,1,0:T(8,128)}, u32[]{:S(2)}, u32[]{:S(2)}) async-start(f32[16,4,8,128]{3,2,1,0:T(8,128)} %bitcast.7), calls=%async_computation | async-start | bytes 524288 | tf_op jit(solution)/shard_map/all_to_all | solution.py:61
  32.8 8.2 %collective-permute-start.5 = (f32[8,128]{1,0:T(8,128)S(1)}, f32[8,128]{1,0:T(8,128)S(1)}, u32[]{:S(2)}, u32[]{:S(2)}) collective-permute-start(f32[8,128]{1,0:T(8,128)S(1)} %collective-permute-done.4), channel_id=1, source_target_pairs={{0,2},{2,0},{1,3},{3,1},{4,6},{6,4},{5,7},{7,5},{8,10},{10,8},{9,1... | collective-permute-start | bytes 12296 | tf_op jit(solution)/shard_map/ppermute | solution.py:34
  50.3 8.1 %collective-permute-start.6 = (f32[16,4,8,128]{3,2,1,0:T(8,128)}, f32[16,4,8,128]{3,2,1,0:T(8,128)S(1)}, u32[]{:S(2)}, u32[]{:S(2)}) collective-permute-start(f32[16,4,8,128]{3,2,1,0:T(8,128)} %all-to-all-done), channel_id=1, source_target_pairs={{0,16},{16,0},{1,17},{17,1},{2,18},{18,2},{3,19},{19,3},{4,20},{20... | collective-permute-start | bytes 786440 | tf_op jit(solution)/shard_map/ppermute | solution.py:34
  238.7 26.2 %collective-permute-start.11 = (f32[8,128]{1,0:T(8,128)S(1)}, f32[8,128]{1,0:T(8,128)S(1)}, u32[]{:S(2)}, u32[]{:S(2)}) collective-permute-start(f32[8,128]{1,0:T(8,128)S(1)} %rev.7), channel_id=1, source_target_pairs={{0,1},{1,0},{2,3},{3,2},{4,5},{5,4},{6,7},{7,6},{8,9},{9,8},{10,11... | collective-permute-start | bytes 12296 | tf_op jit(solution)/shard_map/ppermute | solution.py:34
  239.0 27.1 %collective-permute-start.10 = (f32[8,1,128]{1,2,0:T(8,128)}, f32[8,1,128]{1,2,0:T(8,128)}, u32[]{:S(2)}, u32[]{:S(2)}) collective-permute-start(f32[8,1,128]{1,2,0:T(8,128)} %get-tuple-element.630), channel_id=1, source_target_pairs={{4,0},{8,4},{12,8},{5,1},{9,5},{13,9},{6,2},{10,6},{14,10},{7,3},{... | collective-permute-start | bytes 12296 | tf_op jit(solution)/shard_map/ppermute | solution.py:20
  242.4 17.6 %copy-start.4 = (f32[8,16384]{1,0:T(8,128)S(1)}, f32[8,16384]{1,0:T(8,128)}, u32[]{:S(2)}) copy-start(f32[8,16384]{1,0:T(8,128)} %get-tuple-element.420) | copy-start | bytes 1572868
  243.5 24.0 %all-to-all-start.1 = ((bf16[16,4,8,128]{3,1,2,0:T(4,128)(2,1)}), bf16[16,4,8,128]{3,1,2,0:T(4,128)(2,1)S(1)}, u32[]{:S(2)}, u32[]{:S(2)}) async-start(bf16[16,4,8,128]{3,1,2,0:T(4,128)(2,1)} %copy.141), calls=%async_computation.1 | async-start | bytes 262144 | tf_op jit(solution)/shard_map/all_to_all | solution.py:67
  248.8 39.2 %all-reduce.5.cloned.1.call-start = ((), (), s32[]{:S(2)}) async-start(), calls=%async_computation.2 | async-start | bytes 524288 | tf_op jit(solution)/shard_map/psum | solution.py:232
  249.4 39.9 %collective-permute-start.9 = (f32[8,1,128]{1,2,0:T(8,128)}, f32[8,1,128]{1,2,0:T(8,128)}, u32[]{:S(2)}, u32[]{:S(2)}) collective-permute-start(f32[8,1,128]{1,2,0:T(8,128)} %get-tuple-element.628), channel_id=1, source_target_pairs={{0,4},{4,8},{8,12},{1,5},{5,9},{9,13},{2,6},{6,10},{10,14},{3,7},{... | collective-permute-start | bytes 12296 | tf_op jit(solution)/shard_map/ppermute | solution.py:18
  252.5 36.8 %collective-permute-start.7 = (f32[8,128,1]{1,2,0:T(1,128)S(1)}, f32[8,128,1]{1,2,0:T(1,128)S(1)}, u32[]{:S(2)}, u32[]{:S(2)}) collective-permute-start(f32[8,128,1]{1,2,0:T(1,128)S(1)} %get-tuple-element.626), channel_id=1, source_target_pairs={{1,0},{2,1},{3,2},{0,3},{5,4},{6,5},{7,6},{4,7},{9,8},{10,9},{11,1... | collective-permute-start | bytes 12296 | tf_op jit(solution)/shard_map/ppermute | solution.py:20
  256.0 33.4 %collective-permute-start.8 = (f32[8,128,1]{1,2,0:T(1,128)S(1)}, f32[8,128,1]{1,2,0:T(1,128)S(1)}, u32[]{:S(2)}, u32[]{:S(2)}) collective-permute-start(f32[8,128,1]{1,2,0:T(1,128)S(1)} %get-tuple-element.627), channel_id=1, source_target_pairs={{0,1},{1,2},{2,3},{3,0},{4,5},{5,6},{6,7},{7,4},{8,9},{9,10},{10,1... | collective-permute-start | bytes 12296 | tf_op jit(solution)/shard_map/ppermute | solution.py:18
  264.8 116.3 %all-reduce.7.cloned.1.call-start = ((), (), s32[]{:S(2)}) async-start(), calls=%async_computation.3 | async-start | bytes 524288 | tf_op jit(solution)/shard_map/psum | solution.py:231
  264.9 4.6 %collective-permute-start.12 = (f32[8,128]{1,0:T(8,128)S(1)}, f32[8,128]{1,0:T(8,128)S(1)}, u32[]{:S(2)}, u32[]{:S(2)}) collective-permute-start(f32[8,128]{1,0:T(8,128)S(1)} %collective-permute-done.11), channel_id=1, source_target_pairs={{0,2},{2,0},{1,3},{3,1},{4,6},{6,4},{5,7},{7,5},{8,10},{10,8},{9,1... | collective-permute-start | bytes 12296 | tf_op jit(solution)/shard_map/ppermute | solution.py:34
  267.5 20.6 %collective-permute-start.13 = (bf16[16,4,8,128]{3,1,2,0:T(4,128)(2,1)S(1)}, bf16[16,4,8,128]{3,1,2,0:T(4,128)(2,1)S(1)}, u32[]{:S(2)}, u32[]{:S(2)}) collective-permute-start(bf16[16,4,8,128]{3,1,2,0:T(4,128)(2,1)S(1)} %all-to-all-done.1), channel_id=1, source_target_pairs={{0,16},{16,0},{1,17},{17,1},{2,18},{18,2},{3,19},{19,3},{4,20},{20... | collective-permute-start | bytes 393224 | tf_op jit(solution)/shard_map/ppermute | solution.py:34
  (74 other events, 162.1 us)
Sparse Core Ops, SparseCore 0:
  265.0 23.0 all-reduce.4
  291.4 89.6 all-reduce.6
